TPU v7x, 32 devices: a whole 2x2x4 slice. The times are simulated.
32 devices in a mesh: space: 4 (over y, x), orb: 8 (over z, core).
Axes of the slice: x: 2, y: 2, z: 4, core: 2. Of those that a mesh axis runs over, the one named last changes fastest.
Arguments:
- orbitals: float32 [16, 16, 32, 1024], P('space', None, None, 'orb'), may hold values from -6 to 6
- potential: float32 [16, 16, 32], P('space'), may hold values from 0 to 2
Outputs:
- updated: float32 [16, 16, 32, 1024], P('space', None, None, 'orb')
All inputs are finite; a program needn't handle non-finite values.
Results may differ from a plain program's by a relative error of at most 0.00007.
Values sent between devices are 32-bit elements; how exact they have to be, the bound alone decides.
A program may use at most 64 MiB of HBM per device.

v0:
```python
import jax
import jax.numpy as jnp
from jax import lax
from jax.sharding import PartitionSpec as P

PANEL = 512
DEGREE = 4
STENCIL = (-205.0 / 72.0, 8.0 / 5.0, -1.0 / 5.0, 8.0 / 315.0, -1.0 / 560.0)
SHIFT_MID = 7.25
HALF_WIDTH = 4.75


def padded_2(shard, sides, width):
    for axis, dim in sides:
        count, length = (lax.axis_size(axis), shard.shape[dim])
        up = [(i, (i + 1) % count) for i in range(count)]
        down = [(j, i) for i, j in up]
        last = lax.slice_in_dim(shard, length - width, length, axis=dim)
        leading = lax.slice_in_dim(shard, 0, width, axis=dim)
        before = lax.ppermute(last, axis, up)
        after = lax.ppermute(leading, axis, down)
        shard = jnp.concatenate([before, shard, after], axis=dim)
    return shard


def hamilton(field, potential):
    planes = field.shape[0]
    padded = padded_2(field, (("space", 0),), 4)
    laplace = 3.0 * STENCIL[0] * field
    for offset in range(1, 5):
        upper = padded[4 + offset : 4 + offset + planes]
        below = padded[4 - offset : 4 - offset + planes]
        laplace = laplace + STENCIL[offset] * (upper + below)
    for axis in (1, 2):
        for offset in range(1, 5):
            laplace = laplace + STENCIL[offset] * (
                jnp.roll(field, offset, axis) + jnp.roll(field, -offset, axis)
            )
    return -0.5 * laplace + potential[..., None] * field


def chebyshev(block, potential):
    before = block
    current = (hamilton(block, potential) - SHIFT_MID * block) / HALF_WIDTH
    for order in range(DEGREE - 1):
        following = 2.0 * (hamilton(current, potential) - SHIFT_MID * current) / HALF_WIDTH - before
        before, current = (current, following)
    return current


def per_device(orbitals, potential):
    highest = lax.Precision.HIGHEST
    filtered = chebyshev(orbitals, potential)
    planes, rows_y, rows_z, columns = filtered.shape
    local_points = planes * rows_y * rows_z
    points = local_points * lax.axis_size("space")
    panel_dev = PANEL // lax.axis_size("orb")
    flat = filtered.reshape(local_points, columns)
    panel_own = flat[:, :panel_dev]
    trailing = flat[:, panel_dev:]
    panel = lax.all_gather(panel_own, "orb", axis=1, tiled=True)
    coupling_part = jnp.dot(panel.T, trailing, precision=highest)
    gram_part = jnp.dot(panel.T, panel, precision=highest)
    gram_full, coupling = lax.psum((gram_part, coupling_part), "space")
    gram_full = gram_full / points
    coupling = coupling / points
    lower_factor = jnp.linalg.cholesky(gram_full)
    identity = jnp.eye(PANEL, dtype=jnp.float32)
    inverse = lax.linalg.triangular_solve(lower_factor, identity, left_side=True, lower=True)
    start = lax.axis_index("orb") * panel_dev
    own_rows = lax.dynamic_slice_in_dim(inverse, start, panel_dev, 0)
    ortho_own = jnp.dot(panel, own_rows.T, precision=highest)
    middle = jnp.dot(inverse, coupling, precision=highest)
    project = jnp.dot(inverse.T, middle, precision=highest)
    trailing_new = trailing - jnp.dot(panel, project, precision=highest)
    joined = jnp.concatenate([ortho_own, trailing_new], axis=1)
    return joined.reshape(planes, rows_y, rows_z, columns)


def solution(mesh):
    placed = (P("space", None, None, "orb"), P("space", None, None))
    return jax.shard_map(
        per_device,
        mesh=mesh,
        in_specs=placed,
        out_specs=P("space", None, None, "orb"),
        check_vma=False,
    )
```

profile of v0, /device:TPU:0, one launch (start us, length us, event | category | flops | bytes accessed | tf_op | source)
XLA Modules:
  0.0 514.7 jit_solution(1693416008679827727)
XLA Ops:
  21.2 13.6 %collective-permute-done.1 = f32[4,16,32,128]{3,2,1,0:T(8,128)S(1)} collective-permute-done((f32[4,16,32,128]{3,2,1,0:T(8,128)}, f32[4,16,32,128]{3,2,1,0:T(8,128)S(1)}, u32[]{:S(2)}, u32[]{:S(2)}) %collective-permute-start.1) | collective-permute-done | bytes 1048608 | tf_op jit(solution)/shard_map/ppermute | solution.py:20
  35.0 21.6 %collective-permute-done = f32[4,16,32,128]{3,2,1,0:T(8,128)S(1)} collective-permute-done((f32[4,16,32,128]{3,2,1,0:T(8,128)}, f32[4,16,32,128]{3,2,1,0:T(8,128)S(1)}, u32[]{:S(2)}, u32[]{:S(2)}) %collective-permute-start) | collective-permute-done | bytes 1048608 | tf_op jit(solution)/shard_map/ppermute | solution.py:21
  56.6 5.3 %broadcast_multiply_fusion.1 = (f32[4,16,32,128]{3,2,1,0:T(8,128)S(1)}, f32[4,16,32,128]{3,2,1,0:T(8,128)S(1)}) fusion(f32[4,16,32,128]{3,2,1,0:T(8,128)S(1)} %copy-done, f32[4,16,32]{2,1,0:T(8,128)S(1)} %copy-done.12, f32[4,16,4,128]{3,2,1,0:T(4,128)} %get-tuple-element.156, f32[4,16,28,128]{3,2,1,0:T(8,128)S(1)} %get-tuple-element.158, ...), kind=kLoop, calls=%fused_computation.211 | loop fusion | flops 15466496 | bytes 28319744 | tf_op jit(solution)/shard_map/div | solution.py:44
  72.9 22.7 %collective-permute-done.2 = f32[4,16,32,128]{3,2,1,0:T(8,128)S(1)} collective-permute-done((f32[4,16,32,128]{3,2,1,0:T(8,128)S(1)}, f32[4,16,32,128]{3,2,1,0:T(8,128)S(1)}, u32[]{:S(2)}, u32[]{:S(2)}) %collective-permute-start.2) | collective-permute-done | bytes 1048608 | tf_op jit(solution)/shard_map/ppermute | solution.py:21
  95.6 20.6 %collective-permute-done.3 = f32[4,16,32,128]{3,2,1,0:T(8,128)S(1)} collective-permute-done((f32[4,16,32,128]{3,2,1,0:T(8,128)S(1)}, f32[4,16,32,128]{3,2,1,0:T(8,128)S(1)}, u32[]{:S(2)}, u32[]{:S(2)}) %collective-permute-start.3) | collective-permute-done | bytes 1048608 | tf_op jit(solution)/shard_map/ppermute | solution.py:20
  117.2 6.9 %multiply_subtract_fusion.2 = f32[4,16,32,128]{3,2,1,0:T(8,128)S(1)} fusion(f32[4,16,32,128]{3,2,1,0:T(8,128)S(1)} %copy-done, f32[4,16,32,128]{3,2,1,0:T(8,128)S(1)} %get-tuple-element.24, f32[4,16,4,128]{3,2,1,0:T(4,128)} %get-tuple-element.122, f32[4,16,28,128]{3,2,1,0:T(8,128)S(1)} %get-tuple-element.124, f32[4,16,28,128]{3,2,1,0:T(8,128)S(1)} %get-tuple-element.123, ...), kind=kLoop, calls=%fused_computation.201 | loop fusion | flops 17301504 | bytes 23076864 | tf_op jit(solution)/shard_map/sub | solution.py:46
  135.1 17.0 %collective-permute-done.4 = f32[4,16,32,128]{3,2,1,0:T(8,128)S(1)} collective-permute-done((f32[4,16,32,128]{3,2,1,0:T(8,128)S(1)}, f32[4,16,32,128]{3,2,1,0:T(8,128)S(1)}, u32[]{:S(2)}, u32[]{:S(2)}) %collective-permute-start.4) | collective-permute-done | bytes 1048608 | tf_op jit(solution)/shard_map/ppermute | solution.py:21
  152.1 20.4 %collective-permute-done.5 = f32[4,16,32,128]{3,2,1,0:T(8,128)S(1)} collective-permute-done((f32[4,16,32,128]{3,2,1,0:T(8,128)S(1)}, f32[4,16,32,128]{3,2,1,0:T(8,128)S(1)}, u32[]{:S(2)}, u32[]{:S(2)}) %collective-permute-start.5) | collective-permute-done | bytes 1048608 | tf_op jit(solution)/shard_map/ppermute | solution.py:20
  173.5 6.9 %multiply_subtract_fusion.1 = f32[4,16,32,128]{3,2,1,0:T(8,128)S(1)} fusion(f32[4,16,32,128]{3,2,1,0:T(8,128)S(1)} %multiply_subtract_fusion.2, f32[4,16,4,128]{3,2,1,0:T(4,128)} %get-tuple-element.90, f32[4,16,28,128]{3,2,1,0:T(8,128)S(1)} %get-tuple-element.92, f32[4,16,28,128]{3,2,1,0:T(8,128)S(1)} %get-tuple-element.91, ...), kind=kLoop, calls=%fused_computation.200 | loop fusion | flops 17563648 | bytes 22028288 | tf_op jit(solution)/shard_map/sub | solution.py:46
  190.4 18.2 %collective-permute-done.6 = f32[4,16,32,128]{3,2,1,0:T(8,128)S(1)} collective-permute-done((f32[4,16,32,128]{3,2,1,0:T(8,128)S(1)}, f32[4,16,32,128]{3,2,1,0:T(8,128)S(1)}, u32[]{:S(2)}, u32[]{:S(2)}) %collective-permute-start.6) | collective-permute-done | bytes 1048608 | tf_op jit(solution)/shard_map/ppermute | solution.py:21
  208.7 19.4 %collective-permute-done.7 = f32[4,16,32,128]{3,2,1,0:T(8,128)S(1)} collective-permute-done((f32[4,16,32,128]{3,2,1,0:T(8,128)S(1)}, f32[4,16,32,128]{3,2,1,0:T(8,128)S(1)}, u32[]{:S(2)}, u32[]{:S(2)}) %collective-permute-start.7) | collective-permute-done | bytes 1048608 | tf_op jit(solution)/shard_map/ppermute | solution.py:20
  229.1 6.8 %multiply_subtract_fusion = f32[4,16,32,128]{3,2,1,0:T(8,128)S(1)} fusion(f32[4,16,32,128]{3,2,1,0:T(8,128)S(1)} %multiply_subtract_fusion.2, f32[4,16,32,128]{3,2,1,0:T(8,128)S(1)} %multiply_subtract_fusion.1, f32[4,16,4,128]{3,2,1,0:T(4,128)} %get-tuple-element.58, f32[4,16,28,128]{3,2,1,0:T(8,128)S(1)} %get-tuple-element.60, ...), kind=kLoop, calls=%fused_computation.199 | loop fusion | flops 17301504 | bytes 22028288 | tf_op jit(solution)/shard_map/sub | solution.py:46
  237.5 47.5 %all-gather.2.cloned.1.call-done = f32[2048,512]{0,1:T(8,128)} async-done(((f32[2048,64]{0,1:T(8,128)}), f32[2048,512]{0,1:T(8,128)}) %all-gather.2.cloned.1.call-update) | async-done | bytes 4194320 | tf_op jit(solution)/shard_map/all_gather | solution.py:61
  285.0 10.7 %fusion.224 = f32[512,512]{0,1:T(8,128)} fusion(f32[2048,512]{0,1:T(8,128)} %all-gather.2.cloned.1.call-done), kind=kOutput, calls=%fused_computation.337 | convolution fusion | flops 6442450944 | bytes 5242880 | tf_op jit(solution)/shard_map/dot_general | solution.py:63
  303.0 51.0 %all-reduce.4.cloned.1.call-done = (f32[512,64]{0,1:T(8,128)}, f32[512,512]{0,1:T(8,128)}) async-done(((f32[512,64]{0,1:T(8,128)}, f32[512,512]{0,1:T(8,128)}), (f32[512,64]{0,1:T(8,128)}, f32[512,512]{0,1:T(8,128)})) %all-reduce.4.cloned.1.call-update) | async-done | bytes 1179664 | tf_op jit(solution)/shard_map/psum | solution.py:64
  356.0 11.7 %cholesky.104 = f32[128,128]{1,0:T(8,128)S(1)} custom-call(f32[128,128]{1,0:T(8,128)S(1)} %cholesky.266), custom_call_target="Cholesky" | custom-call | tf_op jit(solution)/shard_map/jit(cholesky)/cholesky | solution.py:67
  367.9 9.8 %custom-call.30 = f32[1,128,128]{1,2,0:T(8,128)S(1)} custom-call(f32[1,128,128]{2,1,0:T(8,128)S(1)} %get-tuple-element.168), custom_call_target="InvertDiagBlocksLowerTriangular" | custom-call | tf_op jit(solution)/shard_map/jit(cholesky)/cholesky | solution.py:67
  378.4 11.9 %cholesky.217 = f32[128,128]{1,0:T(8,128)S(1)} custom-call(f32[128,128]{1,0:T(8,128)S(1)} %cholesky.270), custom_call_target="Cholesky" | custom-call | tf_op jit(solution)/shard_map/jit(cholesky)/cholesky | solution.py:67
  390.3 9.8 %custom-call.31 = f32[1,128,128]{1,2,0:T(8,128)S(1)} custom-call(f32[1,128,128]{2,1,0:T(8,128)S(1)} %get-tuple-element.165), custom_call_target="InvertDiagBlocksLowerTriangular" | custom-call | tf_op jit(solution)/shard_map/jit(cholesky)/cholesky | solution.py:67
  400.8 12.3 %cholesky.238 = f32[128,128]{1,0:T(8,128)} custom-call(f32[128,128]{1,0:T(8,128)S(1)} %cholesky.275), custom_call_target="Cholesky" | custom-call | tf_op jit(solution)/shard_map/jit(cholesky)/cholesky | solution.py:67
  415.4 11.3 %custom-call.32 = f32[1,128,128]{1,2,0:T(8,128)} custom-call(f32[1,128,128]{2,1,0:T(8,128)} %get-tuple-element.162), custom_call_target="InvertDiagBlocksLowerTriangular" | custom-call | tf_op jit(solution)/shard_map/jit(cholesky)/cholesky | solution.py:67
  428.1 11.9 %cholesky.255 = f32[128,128]{1,0:T(8,128)S(1)} custom-call(f32[128,128]{1,0:T(8,128)S(1)} %convolution_subtract_fusion.6), custom_call_target="Cholesky" | custom-call | tf_op jit(solution)/shard_map/jit(cholesky)/cholesky | solution.py:67
  444.2 10.8 %while.1 = (s32[]{:T(128)}, f32[512,512]{1,0:T(8,128)S(1)}, s32[4,2]{0,1:T(2,128)S(1)}, f32[4,128,128]{2,1,0:T(8,128)}, s32[]{:T(128)}) while((s32[]{:T(128)}, f32[512,512]{1,0:T(8,128)S(1)}, s32[4,2]{0,1:T(2,128)S(1)}, f32[4,128,128]{2,1,0:T(8,128)}, s32[]{:T(128)}) %tuple.94), condition=%wide.while_cond, body=%wide.while_body.sunk | while | flops 2 | bytes 132705 | solution.py:69
  455.0 40.1 %custom-call.33 = f32[4,128,128]{1,2,0:T(8,128)S(1)} custom-call(f32[4,128,128]{2,1,0:T(8,128)} %get-tuple-element.12), custom_call_target="InvertDiagBlocksLowerTriangular" | custom-call | tf_op jit(solution)/shard_map/triangular_solve | solution.py:69
  (166 shorter events, 90.2 us)
Async XLA Ops:
  6.5 5.8 %copy-start = (f32[4,16,32,128]{3,2,1,0:T(8,128)S(1)}, f32[4,16,32,128]{3,2,1,0:T(8,128)}, u32[]{:S(2)}) copy-start(f32[4,16,32,128]{3,2,1,0:T(8,128)} %param.2) | copy-start | bytes 3145732
  6.5 278.4 %all-gather.2.cloned.1.call-start = ((), (), s32[]{:S(2)}) async-start(), calls=%async_computation | async-start | bytes 4718592 | tf_op jit(solution)/shard_map/all_gather | solution.py:61
  6.5 28.2 %collective-permute-start.1 = (f32[4,16,32,128]{3,2,1,0:T(8,128)}, f32[4,16,32,128]{3,2,1,0:T(8,128)S(1)}, u32[]{:S(2)}, u32[]{:S(2)}) collective-permute-start(f32[4,16,32,128]{3,2,1,0:T(8,128)} %param.2), channel_id=1, source_target_pairs={{0,8},{8,16},{16,24},{24,0},{1,9},{9,17},{17,25},{25,1},{2,10},{10... | collective-permute-start | bytes 3145736 | tf_op jit(solution)/shard_map/ppermute | solution.py:20
  9.5 47.0 %collective-permute-start = (f32[4,16,32,128]{3,2,1,0:T(8,128)}, f32[4,16,32,128]{3,2,1,0:T(8,128)S(1)}, u32[]{:S(2)}, u32[]{:S(2)}) collective-permute-start(f32[4,16,32,128]{3,2,1,0:T(8,128)} %param.2), channel_id=1, source_target_pairs={{8,0},{16,8},{24,16},{0,24},{9,1},{17,9},{25,17},{1,25},{10,2},{18... | collective-permute-start | bytes 3145736 | tf_op jit(solution)/shard_map/ppermute | solution.py:21
  16.4 4.3 copy-start.12
  69.5 26.0 %collective-permute-start.2 = (f32[4,16,32,128]{3,2,1,0:T(8,128)S(1)}, f32[4,16,32,128]{3,2,1,0:T(8,128)S(1)}, u32[]{:S(2)}, u32[]{:S(2)}) collective-permute-start(f32[4,16,32,128]{3,2,1,0:T(8,128)S(1)} %get-tuple-element.23), channel_id=1, source_target_pairs={{8,0},{16,8},{24,16},{0,24},{9,1},{17,9},{25,17},{1,25},{10,2},{18... | collective-permute-start | bytes 3145736 | tf_op jit(solution)/shard_map/ppermute | solution.py:21
  71.0 45.2 %collective-permute-start.3 = (f32[4,16,32,128]{3,2,1,0:T(8,128)S(1)}, f32[4,16,32,128]{3,2,1,0:T(8,128)S(1)}, u32[]{:S(2)}, u32[]{:S(2)}) collective-permute-start(f32[4,16,32,128]{3,2,1,0:T(8,128)S(1)} %get-tuple-element.23), channel_id=1, source_target_pairs={{0,8},{8,16},{16,24},{24,0},{1,9},{9,17},{17,25},{25,1},{2,10},{10... | collective-permute-start | bytes 3145736 | tf_op jit(solution)/shard_map/ppermute | solution.py:20
  95.6 20.6 %copy-start.10 = (f32[4,16,32,128]{3,2,1,0:T(8,128)}, f32[4,16,32,128]{3,2,1,0:T(8,128)S(1)}, u32[]{:S(2)}) copy-start(f32[4,16,32,128]{3,2,1,0:T(8,128)S(1)} %collective-permute-done.2) | copy-start | bytes 3145732
  116.2 1.0 copy-start.11
  126.0 26.0 %collective-permute-start.4 = (f32[4,16,32,128]{3,2,1,0:T(8,128)S(1)}, f32[4,16,32,128]{3,2,1,0:T(8,128)S(1)}, u32[]{:S(2)}, u32[]{:S(2)}) collective-permute-start(f32[4,16,32,128]{3,2,1,0:T(8,128)S(1)} %multiply_subtract_fusion.2), channel_id=1, source_target_pairs={{8,0},{16,8},{24,16},{0,24},{9,1},{17,9},{25,17},{1,25},{10,2},{18... | collective-permute-start | bytes 3145736 | tf_op jit(solution)/shard_map/ppermute | solution.py:21
  128.3 44.2 %collective-permute-start.5 = (f32[4,16,32,128]{3,2,1,0:T(8,128)S(1)}, f32[4,16,32,128]{3,2,1,0:T(8,128)S(1)}, u32[]{:S(2)}, u32[]{:S(2)}) collective-permute-start(f32[4,16,32,128]{3,2,1,0:T(8,128)S(1)} %multiply_subtract_fusion.2), channel_id=1, source_target_pairs={{0,8},{8,16},{16,24},{24,0},{1,9},{9,17},{17,25},{25,1},{2,10},{10... | collective-permute-start | bytes 3145736 | tf_op jit(solution)/shard_map/ppermute | solution.py:20
  152.1 20.4 %copy-start.7 = (f32[4,16,32,128]{3,2,1,0:T(8,128)}, f32[4,16,32,128]{3,2,1,0:T(8,128)S(1)}, u32[]{:S(2)}) copy-start(f32[4,16,32,128]{3,2,1,0:T(8,128)S(1)} %collective-permute-done.4) | copy-start | bytes 3145732
  172.5 1.0 copy-start.9
  182.6 26.0 %collective-permute-start.6 = (f32[4,16,32,128]{3,2,1,0:T(8,128)S(1)}, f32[4,16,32,128]{3,2,1,0:T(8,128)S(1)}, u32[]{:S(2)}, u32[]{:S(2)}) collective-permute-start(f32[4,16,32,128]{3,2,1,0:T(8,128)S(1)} %multiply_subtract_fusion.1), channel_id=1, source_target_pairs={{8,0},{16,8},{24,16},{0,24},{9,1},{17,9},{25,17},{1,25},{10,2},{18... | collective-permute-start | bytes 3145736 | tf_op jit(solution)/shard_map/ppermute | solution.py:21
  184.1 44.0 %collective-permute-start.7 = (f32[4,16,32,128]{3,2,1,0:T(8,128)S(1)}, f32[4,16,32,128]{3,2,1,0:T(8,128)S(1)}, u32[]{:S(2)}, u32[]{:S(2)}) collective-permute-start(f32[4,16,32,128]{3,2,1,0:T(8,128)S(1)} %multiply_subtract_fusion.1), channel_id=1, source_target_pairs={{0,8},{8,16},{16,24},{24,0},{1,9},{9,17},{17,25},{25,1},{2,10},{10... | collective-permute-start | bytes 3145736 | tf_op jit(solution)/shard_map/ppermute | solution.py:20
  190.2 38.9 %copy-start.13 = (f32[4,16,32]{2,1,0:T(8,128)S(1)}, f32[4,16,32]{2,1,0:T(8,128)}, u32[]{:S(2)}) copy-start(f32[4,16,32]{2,1,0:T(8,128)} %param.3) | copy-start | bytes 24580
  208.7 19.4 %copy-start.6 = (f32[4,16,32,128]{3,2,1,0:T(8,128)}, f32[4,16,32,128]{3,2,1,0:T(8,128)S(1)}, u32[]{:S(2)}) copy-start(f32[4,16,32,128]{3,2,1,0:T(8,128)S(1)} %collective-permute-done.6) | copy-start | bytes 3145732
  237.4 116.6 %all-reduce.4.cloned.1.call-start = ((), (), s32[]{:S(2)}) async-start(), calls=%async_computation.1 | async-start | bytes 2359296 | tf_op jit(solution)/shard_map/psum | solution.py:64
  285.0 10.7 %copy-start.1 = (f32[2048,512]{0,1:T(8,128)S(1)}, f32[2048,512]{0,1:T(8,128)}, u32[]{:S(2)}) copy-start(f32[2048,512]{0,1:T(8,128)} %all-gather.2.cloned.1.call-done) | copy-start | bytes 12582916
  354.0 1.8 copy-start.3
  413.1 82.3 %copy-start.4 = (f32[512,512]{1,0:T(8,128)S(1)}, f32[512,512]{1,0:T(8,128)}, u32[]{:S(2)}) copy-start(f32[512,512]{1,0:T(8,128)} %fusion.125) | copy-start | bytes 3145732
  497.1 1.2 copy-start.14
  498.2 2.2 copy-start.2
  500.4 2.9 copy-start.5
  (1 other events, 1.0 us)
Sparse Core Ops, SparseCore 0:
  237.5 47.3 all-gather.1
  300.8 53.1 all-reduce.3
where the time goes:
time: 522 us; the launch traced here: 515 us
  waiting for transfers between devices  252 us (48%)
  other arithmetic  152 us (29%)
  local copies, waits for them, and re-layouts  54.5 us (10%)
  matrix products  29 us (6%)
  between operations  17 us (3%)
  starting transfers between devices  10.5 us (2%)
    another operation x14, other arithmetic, per_device(): lower_factor = jnp.linalg.cholesky(gram_full)  82.5 us
    ppermute x4, waiting for transfers between devices, padded_2(): after = lax.ppermute(leading, axis, down)  79.4 us
    ppermute x4, waiting for transfers between devices, padded_2(): before = lax.ppermute(last, axis, up)  74 us
    psum x1, waiting for transfers between devices, per_device(): gram_full, coupling = lax.psum((gram_part, coupling_part), 'space')  51 us
    all_gather x1, waiting for transfers between devices, per_device(): panel = lax.all_gather(panel_own, 'orb', axis=1, tiled=True)  47.5 us
    another operation x4, other arithmetic, per_device(): lax.linalg.triangular_solve(lower_factor, identity, left_side=True, lower...  40.3 us
    slice x64, local copies, waits for them, and re-layouts, hamilton(): jnp.roll(field, offset, axis) + jnp.roll(field, -offset, axis)  35.9 us
    sub x3, other arithmetic, chebyshev(): 2.0 * (hamilton(current, potential) - SHIFT_MID * current) / HALF_WIDTH  20.7 us
  transfers between devices with their start and end apart: 10, of which 10 were waited for; matrix products, arithmetic and copies ran while one was open for 5% of the time, Pallas kernels for 0%

commit v1 on v0

--- a/solution.py
+++ b/solution.py
@@ -49,6 +49,26 @@
 
 
 def per_device(orbitals, potential):
+
+    def series_arrange(content):
+        axis_key = "orb"
+        low = lax.psum(1, axis_key)
+        step_out = lax.axis_index(axis_key)
+        finding, x_new, lower = (low, step_out, content.shape[1])
+        oldest = jnp.zeros(
+            [h * finding if ix == 1 else h for ix, h in enumerate(content.shape)], content.dtype
+        )
+        top = lax.dynamic_update_slice_in_dim(oldest, content, x_new * lower, axis=1)
+        for hop_no in range(1, finding):
+            built = range(finding)
+            v_next = map(lambda ix: (ix, (ix + 1) % finding), built)
+            piece_out = list(v_next)
+            content = lax.ppermute(content, axis_key, piece_out)
+            top = lax.dynamic_update_slice_in_dim(
+                top, content, (x_new - hop_no) % finding * lower, axis=1
+            )
+        return top
+
     highest = lax.Precision.HIGHEST
     filtered = chebyshev(orbitals, potential)
     planes, rows_y, rows_z, columns = filtered.shape
@@ -58,7 +78,7 @@
     flat = filtered.reshape(local_points, columns)
     panel_own = flat[:, :panel_dev]
     trailing = flat[:, panel_dev:]
-    panel = lax.all_gather(panel_own, "orb", axis=1, tiled=True)
+    panel = series_arrange(panel_own)
     coupling_part = jnp.dot(panel.T, trailing, precision=highest)
     gram_part = jnp.dot(panel.T, panel, precision=highest)
     gram_full, coupling = lax.psum((gram_part, coupling_part), "space")

time: 522 us -> 607 us (1.16)
  local copies, waits for them, and re-layouts: 54.5 us -> 119 us
  waiting for transfers between devices: 252 us -> 268 us
    ppermute x0 -> x7, waiting for transfers between devices: none -> 62.7 us  [series_arrange(): content = lax.ppermute(content, axis_key, piece_out)]
    dynamic_update_slice x0 -> x8, local copies, waits for them, and re-layouts: none -> 48.5 us  [the longest x7 42.6 us: series_arrange(): lax.dynamic_update_slice_in_dim(top, content, (x_new - hop_no) % finding...]
    all_gather x1 -> x0, waiting for transfers between devices: 47.5 us -> none  [per_device(): panel = lax.all_gather(panel_own, 'orb', axis=1, tiled=True)]
    ppermute x0 -> x7, local copies, waits for them, and re-layouts: none -> 9.58 us  [series_arrange(): content = lax.ppermute(content, axis_key, piece_out)]
  transfers between devices with their start and end apart: 10 -> 16, of which waited for: 10 -> 15; matrix products, arithmetic and copies ran while one was open for 5% -> 13% of each run, Pallas kernels for 0% -> 0%
where the time goes in v1:
time: 607 us; the launch traced here: 598 us
  waiting for transfers between devices  268 us (44%)
  other arithmetic  152 us (25%)
  local copies, waits for them, and re-layouts  119 us (20%)
  matrix products  30.9 us (5%)
  between operations  16.8 us (3%)
  starting transfers between devices  10.9 us (2%)
    another operation x14, other arithmetic, per_device(): lower_factor = jnp.linalg.cholesky(gram_full)  82.6 us
    ppermute x4, waiting for transfers between devices, padded_2(): after = lax.ppermute(leading, axis, down)  79.1 us
    ppermute x4, waiting for transfers between devices, padded_2(): before = lax.ppermute(last, axis, up)  74 us
    ppermute x7, waiting for transfers between devices, series_arrange(): content = lax.ppermute(content, axis_key, piece_out)  62.7 us
    psum x1, waiting for transfers between devices, per_device(): gram_full, coupling = lax.psum((gram_part, coupling_part), 'space')  52.6 us
    dynamic_update_slice x7, local copies, waits for them, and re-layouts, series_arrange(): lax.dynamic_update_slice_in_dim(top, content, (x_new - hop_no) % finding...  42.6 us
    another operation x4, other arithmetic, per_device(): lax.linalg.triangular_solve(lower_factor, identity, left_side=True, lower...  40.3 us
    slice x64, local copies, waits for them, and re-layouts, hamilton(): jnp.roll(field, offset, axis) + jnp.roll(field, -offset, axis)  36 us
  transfers between devices with their start and end apart: 16, of which 15 were waited for; matrix products, arithmetic and copies ran while one was open for 13% of the time, Pallas kernels for 0%

profile of v1, /device:TPU:0, one launch (start us, length us, event | category | flops | bytes accessed | tf_op | source)
XLA Modules:
  0.0 598.1 jit_solution(16869442312271368046)
XLA Ops:
  21.2 13.6 %collective-permute-done.1 = f32[4,16,32,128]{3,2,1,0:T(8,128)S(1)} collective-permute-done((f32[4,16,32,128]{3,2,1,0:T(8,128)}, f32[4,16,32,128]{3,2,1,0:T(8,128)S(1)}, u32[]{:S(2)}, u32[]{:S(2)}) %collective-permute-start.1) | collective-permute-done | bytes 1048608 | tf_op jit(solution)/shard_map/ppermute | solution.py:20
  35.0 21.6 %collective-permute-done = f32[4,16,32,128]{3,2,1,0:T(8,128)S(1)} collective-permute-done((f32[4,16,32,128]{3,2,1,0:T(8,128)}, f32[4,16,32,128]{3,2,1,0:T(8,128)S(1)}, u32[]{:S(2)}, u32[]{:S(2)}) %collective-permute-start) | collective-permute-done | bytes 1048608 | tf_op jit(solution)/shard_map/ppermute | solution.py:21
  73.0 22.7 %collective-permute-done.2 = f32[4,16,32,128]{3,2,1,0:T(8,128)S(1)} collective-permute-done((f32[4,16,32,128]{3,2,1,0:T(8,128)S(1)}, f32[4,16,32,128]{3,2,1,0:T(8,128)S(1)}, u32[]{:S(2)}, u32[]{:S(2)}) %collective-permute-start.2) | collective-permute-done | bytes 1048608 | tf_op jit(solution)/shard_map/ppermute | solution.py:21
  95.6 20.6 %collective-permute-done.3 = f32[4,16,32,128]{3,2,1,0:T(8,128)S(1)} collective-permute-done((f32[4,16,32,128]{3,2,1,0:T(8,128)S(1)}, f32[4,16,32,128]{3,2,1,0:T(8,128)S(1)}, u32[]{:S(2)}, u32[]{:S(2)}) %collective-permute-start.3) | collective-permute-done | bytes 1048608 | tf_op jit(solution)/shard_map/ppermute | solution.py:20
  135.5 16.7 %collective-permute-done.4 = f32[4,16,32,128]{3,2,1,0:T(8,128)S(1)} collective-permute-done((f32[4,16,32,128]{3,2,1,0:T(8,128)S(1)}, f32[4,16,32,128]{3,2,1,0:T(8,128)S(1)}, u32[]{:S(2)}, u32[]{:S(2)}) %collective-permute-start.4) | collective-permute-done | bytes 1048608 | tf_op jit(solution)/shard_map/ppermute | solution.py:21
  152.1 20.4 %collective-permute-done.5 = f32[4,16,32,128]{3,2,1,0:T(8,128)S(1)} collective-permute-done((f32[4,16,32,128]{3,2,1,0:T(8,128)S(1)}, f32[4,16,32,128]{3,2,1,0:T(8,128)S(1)}, u32[]{:S(2)}, u32[]{:S(2)}) %collective-permute-start.5) | collective-permute-done | bytes 1048608 | tf_op jit(solution)/shard_map/ppermute | solution.py:20
  190.6 18.2 %collective-permute-done.6 = f32[4,16,32,128]{3,2,1,0:T(8,128)S(1)} collective-permute-done((f32[4,16,32,128]{3,2,1,0:T(8,128)S(1)}, f32[4,16,32,128]{3,2,1,0:T(8,128)S(1)}, u32[]{:S(2)}, u32[]{:S(2)}) %collective-permute-start.6) | collective-permute-done | bytes 1048608 | tf_op jit(solution)/shard_map/ppermute | solution.py:21
  208.8 19.4 %collective-permute-done.7 = f32[4,16,32,128]{3,2,1,0:T(8,128)S(1)} collective-permute-done((f32[4,16,32,128]{3,2,1,0:T(8,128)S(1)}, f32[4,16,32,128]{3,2,1,0:T(8,128)S(1)}, u32[]{:S(2)}, u32[]{:S(2)}) %collective-permute-start.7) | collective-permute-done | bytes 1048608 | tf_op jit(solution)/shard_map/ppermute | solution.py:20
  237.7 10.6 %collective-permute-done.8 = f32[2048,64]{0,1:T(8,128)S(1)} collective-permute-done((f32[2048,64]{0,1:T(8,128)}, f32[2048,64]{0,1:T(8,128)S(1)}, u32[]{:S(2)}, u32[]{:S(2)}) %collective-permute-start.8) | collective-permute-done | bytes 524320 | tf_op jit(solution)/shard_map/ppermute | solution.py:66
  249.1 10.4 %collective-permute-done.9 = f32[2048,64]{0,1:T(8,128)S(1)} collective-permute-done((f32[2048,64]{0,1:T(8,128)S(1)}, f32[2048,64]{0,1:T(8,128)S(1)}, u32[]{:S(2)}, u32[]{:S(2)}) %collective-permute-start.9) | collective-permute-done | bytes 524320 | tf_op jit(solution)/shard_map/ppermute | solution.py:66
  260.3 10.4 %collective-permute-done.10 = f32[2048,64]{0,1:T(8,128)S(1)} collective-permute-done((f32[2048,64]{0,1:T(8,128)S(1)}, f32[2048,64]{0,1:T(8,128)S(1)}, u32[]{:S(2)}, u32[]{:S(2)}) %collective-permute-start.10) | collective-permute-done | bytes 524320 | tf_op jit(solution)/shard_map/ppermute | solution.py:66
  271.5 10.4 %collective-permute-done.11 = f32[2048,64]{0,1:T(8,128)S(1)} collective-permute-done((f32[2048,64]{0,1:T(8,128)S(1)}, f32[2048,64]{0,1:T(8,128)S(1)}, u32[]{:S(2)}, u32[]{:S(2)}) %collective-permute-start.11) | collective-permute-done | bytes 524320 | tf_op jit(solution)/shard_map/ppermute | solution.py:66
  282.7 10.4 %collective-permute-done.12 = f32[2048,64]{0,1:T(8,128)S(1)} collective-permute-done((f32[2048,64]{0,1:T(8,128)S(1)}, f32[2048,64]{0,1:T(8,128)S(1)}, u32[]{:S(2)}, u32[]{:S(2)}) %collective-permute-start.12) | collective-permute-done | bytes 524320 | tf_op jit(solution)/shard_map/ppermute | solution.py:66
  293.9 10.5 %collective-permute-done.13 = f32[2048,64]{0,1:T(8,128)} collective-permute-done((f32[2048,64]{0,1:T(8,128)S(1)}, f32[2048,64]{0,1:T(8,128)}, u32[]{:S(2)}, u32[]{:S(2)}) %collective-permute-start.13) | collective-permute-done | bytes 524320 | tf_op jit(solution)/shard_map/ppermute | solution.py:66
  365.5 11.5 %fusion.224 = f32[512,512]{0,1:T(8,128)} fusion(f32[2048,512]{1,0:T(8,128)} %dynamic_update_slice.31), kind=kOutput, calls=%fused_computation.337 | convolution fusion | flops 6442450944 | bytes 5242880 | tf_op jit(solution)/shard_map/dot_general | solution.py:83
  382.7 52.6 %all-reduce.4.cloned.1.call-done = (f32[512,64]{0,1:T(8,128)}, f32[512,512]{0,1:T(8,128)}) async-done(((f32[512,64]{0,1:T(8,128)}, f32[512,512]{0,1:T(8,128)}), (f32[512,64]{0,1:T(8,128)}, f32[512,512]{0,1:T(8,128)})) %all-reduce.4.cloned.1.call-update) | async-done | bytes 1179664 | tf_op jit(solution)/shard_map/psum | solution.py:84
  437.3 11.7 %cholesky.104 = f32[128,128]{1,0:T(8,128)S(1)} custom-call(f32[128,128]{1,0:T(8,128)S(1)} %cholesky.266), custom_call_target="Cholesky" | custom-call | tf_op jit(solution)/shard_map/jit(cholesky)/cholesky | solution.py:87
  459.6 12.2 %cholesky.217 = f32[128,128]{1,0:T(8,128)S(1)} custom-call(f32[128,128]{1,0:T(8,128)S(1)} %cholesky.270), custom_call_target="Cholesky" | custom-call | tf_op jit(solution)/shard_map/jit(cholesky)/cholesky | solution.py:87
  471.8 9.8 %custom-call.31 = f32[1,128,128]{1,2,0:T(8,128)S(1)} custom-call(f32[1,128,128]{2,1,0:T(8,128)S(1)} %get-tuple-element.165), custom_call_target="InvertDiagBlocksLowerTriangular" | custom-call | tf_op jit(solution)/shard_map/jit(cholesky)/cholesky | solution.py:87
  482.3 12.3 %cholesky.238 = f32[128,128]{1,0:T(8,128)} custom-call(f32[128,128]{1,0:T(8,128)S(1)} %cholesky.275), custom_call_target="Cholesky" | custom-call | tf_op jit(solution)/shard_map/jit(cholesky)/cholesky | solution.py:87
  496.8 11.3 %custom-call.32 = f32[1,128,128]{1,2,0:T(8,128)} custom-call(f32[1,128,128]{2,1,0:T(8,128)} %get-tuple-element.162), custom_call_target="InvertDiagBlocksLowerTriangular" | custom-call | tf_op jit(solution)/shard_map/jit(cholesky)/cholesky | solution.py:87
  509.6 11.9 %cholesky.255 = f32[128,128]{1,0:T(8,128)S(1)} custom-call(f32[128,128]{1,0:T(8,128)S(1)} %convolution_subtract_fusion.6), custom_call_target="Cholesky" | custom-call | tf_op jit(solution)/shard_map/jit(cholesky)/cholesky | solution.py:87
  525.3 10.2 %while.1 = (s32[]{:T(128)}, f32[512,512]{1,0:T(8,128)S(1)}, s32[4,2]{0,1:T(2,128)S(1)}, f32[4,128,128]{2,1,0:T(8,128)}, s32[]{:T(128)}) while((s32[]{:T(128)}, f32[512,512]{1,0:T(8,128)S(1)}, s32[4,2]{0,1:T(2,128)S(1)}, f32[4,128,128]{2,1,0:T(8,128)}, s32[]{:T(128)}) %tuple.94), condition=%wide.while_cond, body=%wide.while_body.sunk | while | flops 2 | bytes 132705 | solution.py:89
  535.5 40.1 %custom-call.33 = f32[4,128,128]{1,2,0:T(8,128)S(1)} custom-call(f32[4,128,128]{2,1,0:T(8,128)} %get-tuple-element.12), custom_call_target="InvertDiagBlocksLowerTriangular" | custom-call | tf_op jit(solution)/shard_map/triangular_solve | solution.py:89
  (203 shorter events, 192.2 us)
Async XLA Ops:
  6.5 5.8 copy-start
  6.5 428.7 %all-reduce.4.cloned.1.call-start = ((), (), s32[]{:S(2)}) async-start(), calls=%async_computation | async-start | bytes 2359296 | tf_op jit(solution)/shard_map/psum | solution.py:84
  6.5 28.2 %collective-permute-start.1 = (f32[4,16,32,128]{3,2,1,0:T(8,128)}, f32[4,16,32,128]{3,2,1,0:T(8,128)S(1)}, u32[]{:S(2)}, u32[]{:S(2)}) collective-permute-start(f32[4,16,32,128]{3,2,1,0:T(8,128)} %param.2), channel_id=1, source_target_pairs={{0,8},{8,16},{16,24},{24,0},{1,9},{9,17},{17,25},{25,1},{2,10},{10... | collective-permute-start | bytes 3145736 | tf_op jit(solution)/shard_map/ppermute | solution.py:20
  9.5 47.0 %collective-permute-start = (f32[4,16,32,128]{3,2,1,0:T(8,128)}, f32[4,16,32,128]{3,2,1,0:T(8,128)S(1)}, u32[]{:S(2)}, u32[]{:S(2)}) collective-permute-start(f32[4,16,32,128]{3,2,1,0:T(8,128)} %param.2), channel_id=1, source_target_pairs={{8,0},{16,8},{24,16},{0,24},{9,1},{17,9},{25,17},{1,25},{10,2},{18... | collective-permute-start | bytes 3145736 | tf_op jit(solution)/shard_map/ppermute | solution.py:21
  16.4 4.3 copy-start.17
  69.6 26.0 %collective-permute-start.2 = (f32[4,16,32,128]{3,2,1,0:T(8,128)S(1)}, f32[4,16,32,128]{3,2,1,0:T(8,128)S(1)}, u32[]{:S(2)}, u32[]{:S(2)}) collective-permute-start(f32[4,16,32,128]{3,2,1,0:T(8,128)S(1)} %get-tuple-element.23), channel_id=1, source_target_pairs={{8,0},{16,8},{24,16},{0,24},{9,1},{17,9},{25,17},{1,25},{10,2},{18... | collective-permute-start | bytes 3145736 | tf_op jit(solution)/shard_map/ppermute | solution.py:21
  71.0 45.2 %collective-permute-start.3 = (f32[4,16,32,128]{3,2,1,0:T(8,128)S(1)}, f32[4,16,32,128]{3,2,1,0:T(8,128)S(1)}, u32[]{:S(2)}, u32[]{:S(2)}) collective-permute-start(f32[4,16,32,128]{3,2,1,0:T(8,128)S(1)} %get-tuple-element.23), channel_id=1, source_target_pairs={{0,8},{8,16},{16,24},{24,0},{1,9},{9,17},{17,25},{25,1},{2,10},{10... | collective-permute-start | bytes 3145736 | tf_op jit(solution)/shard_map/ppermute | solution.py:20
  95.6 20.6 %copy-start.10 = (f32[4,16,32,128]{3,2,1,0:T(8,128)}, f32[4,16,32,128]{3,2,1,0:T(8,128)S(1)}, u32[]{:S(2)}) copy-start(f32[4,16,32,128]{3,2,1,0:T(8,128)S(1)} %collective-permute-done.2) | copy-start | bytes 3145732
  126.1 26.0 %collective-permute-start.4 = (f32[4,16,32,128]{3,2,1,0:T(8,128)S(1)}, f32[4,16,32,128]{3,2,1,0:T(8,128)S(1)}, u32[]{:S(2)}, u32[]{:S(2)}) collective-permute-start(f32[4,16,32,128]{3,2,1,0:T(8,128)S(1)} %multiply_subtract_fusion.2), channel_id=1, source_target_pairs={{8,0},{16,8},{24,16},{0,24},{9,1},{17,9},{25,17},{1,25},{10,2},{18... | collective-permute-start | bytes 3145736 | tf_op jit(solution)/shard_map/ppermute | solution.py:21
  128.4 44.2 %collective-permute-start.5 = (f32[4,16,32,128]{3,2,1,0:T(8,128)S(1)}, f32[4,16,32,128]{3,2,1,0:T(8,128)S(1)}, u32[]{:S(2)}, u32[]{:S(2)}) collective-permute-start(f32[4,16,32,128]{3,2,1,0:T(8,128)S(1)} %multiply_subtract_fusion.2), channel_id=1, source_target_pairs={{0,8},{8,16},{16,24},{24,0},{1,9},{9,17},{17,25},{25,1},{2,10},{10... | collective-permute-start | bytes 3145736 | tf_op jit(solution)/shard_map/ppermute | solution.py:20
  152.1 20.4 %copy-start.7 = (f32[4,16,32,128]{3,2,1,0:T(8,128)}, f32[4,16,32,128]{3,2,1,0:T(8,128)S(1)}, u32[]{:S(2)}) copy-start(f32[4,16,32,128]{3,2,1,0:T(8,128)S(1)} %collective-permute-done.4) | copy-start | bytes 3145732
  182.8 26.0 %collective-permute-start.6 = (f32[4,16,32,128]{3,2,1,0:T(8,128)S(1)}, f32[4,16,32,128]{3,2,1,0:T(8,128)S(1)}, u32[]{:S(2)}, u32[]{:S(2)}) collective-permute-start(f32[4,16,32,128]{3,2,1,0:T(8,128)S(1)} %multiply_subtract_fusion.1), channel_id=1, source_target_pairs={{8,0},{16,8},{24,16},{0,24},{9,1},{17,9},{25,17},{1,25},{10,2},{18... | collective-permute-start | bytes 3145736 | tf_op jit(solution)/shard_map/ppermute | solution.py:21
  184.2 44.0 %collective-permute-start.7 = (f32[4,16,32,128]{3,2,1,0:T(8,128)S(1)}, f32[4,16,32,128]{3,2,1,0:T(8,128)S(1)}, u32[]{:S(2)}, u32[]{:S(2)}) collective-permute-start(f32[4,16,32,128]{3,2,1,0:T(8,128)S(1)} %multiply_subtract_fusion.1), channel_id=1, source_target_pairs={{0,8},{8,16},{16,24},{24,0},{1,9},{9,17},{17,25},{25,1},{2,10},{10... | collective-permute-start | bytes 3145736 | tf_op jit(solution)/shard_map/ppermute | solution.py:20
  190.4 38.8 %copy-start.18 = (f32[4,16,32]{2,1,0:T(8,128)S(1)}, f32[4,16,32]{2,1,0:T(8,128)}, u32[]{:S(2)}) copy-start(f32[4,16,32]{2,1,0:T(8,128)} %param.3) | copy-start | bytes 24580
  208.8 19.4 %copy-start.6 = (f32[4,16,32,128]{3,2,1,0:T(8,128)}, f32[4,16,32,128]{3,2,1,0:T(8,128)S(1)}, u32[]{:S(2)}) copy-start(f32[4,16,32,128]{3,2,1,0:T(8,128)S(1)} %collective-permute-done.6) | copy-start | bytes 3145732
  237.7 10.6 %collective-permute-start.8 = (f32[2048,64]{0,1:T(8,128)}, f32[2048,64]{0,1:T(8,128)S(1)}, u32[]{:S(2)}, u32[]{:S(2)}) collective-permute-start(f32[2048,64]{0,1:T(8,128)} %copy.11), channel_id=1, source_target_pairs={{0,1},{1,2},{2,3},{3,4},{4,5},{5,6},{6,7},{7,0},{8,9},{9,10},{10,1... | collective-permute-start | bytes 1572872 | tf_op jit(solution)/shard_map/ppermute | solution.py:66
  249.1 10.4 %collective-permute-start.9 = (f32[2048,64]{0,1:T(8,128)S(1)}, f32[2048,64]{0,1:T(8,128)S(1)}, u32[]{:S(2)}, u32[]{:S(2)}) collective-permute-start(f32[2048,64]{0,1:T(8,128)S(1)} %collective-permute-done.8), channel_id=1, source_target_pairs={{0,1},{1,2},{2,3},{3,4},{4,5},{5,6},{6,7},{7,0},{8,9},{9,10},{10,1... | collective-permute-start | bytes 1572872 | tf_op jit(solution)/shard_map/ppermute | solution.py:66
  260.3 10.4 %collective-permute-start.10 = (f32[2048,64]{0,1:T(8,128)S(1)}, f32[2048,64]{0,1:T(8,128)S(1)}, u32[]{:S(2)}, u32[]{:S(2)}) collective-permute-start(f32[2048,64]{0,1:T(8,128)S(1)} %collective-permute-done.9), channel_id=1, source_target_pairs={{0,1},{1,2},{2,3},{3,4},{4,5},{5,6},{6,7},{7,0},{8,9},{9,10},{10,1... | collective-permute-start | bytes 1572872 | tf_op jit(solution)/shard_map/ppermute | solution.py:66
  271.5 10.4 %collective-permute-start.11 = (f32[2048,64]{0,1:T(8,128)S(1)}, f32[2048,64]{0,1:T(8,128)S(1)}, u32[]{:S(2)}, u32[]{:S(2)}) collective-permute-start(f32[2048,64]{0,1:T(8,128)S(1)} %collective-permute-done.10), channel_id=1, source_target_pairs={{0,1},{1,2},{2,3},{3,4},{4,5},{5,6},{6,7},{7,0},{8,9},{9,10},{10,1... | collective-permute-start | bytes 1572872 | tf_op jit(solution)/shard_map/ppermute | solution.py:66
  282.7 10.4 %collective-permute-start.12 = (f32[2048,64]{0,1:T(8,128)S(1)}, f32[2048,64]{0,1:T(8,128)S(1)}, u32[]{:S(2)}, u32[]{:S(2)}) collective-permute-start(f32[2048,64]{0,1:T(8,128)S(1)} %collective-permute-done.11), channel_id=1, source_target_pairs={{0,1},{1,2},{2,3},{3,4},{4,5},{5,6},{6,7},{7,0},{8,9},{9,10},{10,1... | collective-permute-start | bytes 1572872 | tf_op jit(solution)/shard_map/ppermute | solution.py:66
  293.9 10.5 %collective-permute-start.13 = (f32[2048,64]{0,1:T(8,128)S(1)}, f32[2048,64]{0,1:T(8,128)}, u32[]{:S(2)}, u32[]{:S(2)}) collective-permute-start(f32[2048,64]{0,1:T(8,128)S(1)} %collective-permute-done.12), channel_id=1, source_target_pairs={{0,1},{1,2},{2,3},{3,4},{4,5},{5,6},{6,7},{7,0},{8,9},{9,10},{10,1... | collective-permute-start | bytes 1572872 | tf_op jit(solution)/shard_map/ppermute | solution.py:66
  304.4 53.1 %collective-permute-start.14 = (f32[2048,64]{0,1:T(8,128)}, f32[2048,64]{0,1:T(8,128)}, u32[]{:S(2)}, u32[]{:S(2)}) collective-permute-start(f32[2048,64]{0,1:T(8,128)} %collective-permute-done.13), channel_id=1, source_target_pairs={{0,1},{1,2},{2,3},{3,4},{4,5},{5,6},{6,7},{7,0},{8,9},{9,10},{10,1... | collective-permute-start | bytes 1572872 | tf_op jit(solution)/shard_map/ppermute | solution.py:66
  365.5 11.5 %copy-start.1 = (f32[2048,512]{1,0:T(8,128)S(1)}, f32[2048,512]{1,0:T(8,128)}, u32[]{:S(2)}) copy-start(f32[2048,512]{1,0:T(8,128)} %dynamic_update_slice.31) | copy-start | bytes 12582916
  494.6 81.3 %copy-start.4 = (f32[512,512]{1,0:T(8,128)S(1)}, f32[512,512]{1,0:T(8,128)}, u32[]{:S(2)}) copy-start(f32[512,512]{1,0:T(8,128)} %fusion.125) | copy-start | bytes 3145732
  (12 other events, 17.0 us)
Sparse Core Ops, SparseCore 0:
  380.5 54.7 all-reduce.3
